TPU v7x, 128 devices: a whole 4x4x4 slice. The times are simulated.
128 devices in a mesh: ctx: 8 (over y_lo, x), tp: 16 (over z, y_hi, core).
Axes of the slice: x: 4, y: 4 (y_hi: 2, y_lo: 2; y = y_hi * 2 + y_lo), z: 4, core: 2. Of those that a mesh axis runs over, the one named last changes fastest.
Arguments:
- inputs: bfloat16 [6144, 4096], P('ctx', 'tp'), may hold values from -6 to 6
- in_proj: bfloat16 [4096, 3, 4096], P(None, None, 'tp'), may hold values from -0.125 to 0.125
- out_proj: bfloat16 [4096, 4096], P('tp'), may hold values from -0.125 to 0.125
- short_taps: float32 [7, 3, 4096], P(None, None, 'tp'), may hold values from -2.4 to 2.4
- skip_gain: float32 [4096], P('tp'), may hold values from -4 to 4
- long_taps: bfloat16 [128, 256], P(None, 'tp'), may hold values from -1 to 1
- cotangent: bfloat16 [6144, 4096], P('ctx', 'tp'), may hold values from -1.5 to 1.5
Outputs:
- layer_out: bfloat16 [6144, 4096], P('ctx', 'tp')
- grad_inputs: bfloat16 [6144, 4096], P('ctx', 'tp')
- grad_in_proj: float32 [4096, 3, 4096], P('ctx', None, 'tp')
- grad_out_proj: float32 [4096, 4096], P('tp', 'ctx')
- grad_long_taps: float32 [128, 256], P(None, 'tp')
All inputs are finite; a program needn't handle non-finite values.
Results may differ from a plain program's by a relative error of at most 0.014.
Values may be sent and summed in bfloat16 or wider, within the bound.
A program may use at most 128 MiB of HBM per device.

v0:
```python
import jax
import jax.numpy as jnp
from jax import lax
from jax.sharding import PartitionSpec as P

GROUP = 16
LTAPS = 128
STAPS = 7


def shifted(shard, axis, by):
    peers = lax.axis_size(axis)
    pairs = [(i, i + by) for i in range(peers) if 0 <= i + by < peers]
    return lax.ppermute(shard, axis, pairs)


def tap_sum(padded, tap_table, row_count, causal):
    tap_count = tap_table.shape[0]
    running = jnp.zeros((row_count,) + padded.shape[1:], jnp.float32)
    for lag_index in range(tap_count):
        offset = tap_count - 1 - lag_index if causal else lag_index
        running = running + tap_table[lag_index] * padded[offset : offset + row_count].astype(
            jnp.float32
        )
    return running


def make_bands(tap_table):
    tap_count = tap_table.shape[0]
    row_ids = lax.broadcasted_iota(jnp.int32, (tap_count, tap_count, tap_count), 0)
    col_ids = lax.broadcasted_iota(jnp.int32, (tap_count, tap_count, tap_count), 1)
    tap_ids = lax.broadcasted_iota(jnp.int32, (tap_count, tap_count, tap_count), 2)
    lag_ids = row_ids - col_ids
    lower_hot = (lag_ids == tap_ids).astype(jnp.bfloat16)
    upper_hot = (lag_ids + tap_count == tap_ids).astype(jnp.bfloat16)
    lower_band = jnp.einsum(
        "abj,jg->gab", lower_hot, tap_table, preferred_element_type=jnp.float32
    ).astype(jnp.bfloat16)
    upper_band = jnp.einsum(
        "abj,jg->gab", upper_hot, tap_table, preferred_element_type=jnp.float32
    ).astype(jnp.bfloat16)
    return (lower_band, upper_band)


def lag_totals(matrix):
    group_count = matrix.shape[0]
    tap_count = matrix.shape[1]
    flipped = matrix[:, :, ::-1]
    padded = jnp.pad(flipped, ((0, 0), (0, 0), (0, tap_count)))
    flat_rows = padded.reshape(group_count, 2 * tap_count * tap_count)[
        :, : tap_count * (2 * tap_count - 1)
    ]
    return flat_rows.reshape(group_count, tap_count, 2 * tap_count - 1).sum(axis=1)


def local(inputs, in_proj, out_proj, short_taps, skip_gain, long_taps, cotangent):
    token_count = inputs.shape[0]
    model_width = in_proj.shape[0]
    channels_dev = in_proj.shape[2]
    groups_dev = long_taps.shape[1]
    tile_count = token_count // LTAPS
    in_matrix = in_proj.reshape(model_width, 3 * channels_dev)
    inputs_full = lax.all_gather(inputs, "tp", axis=1, tiled=True)
    projected = jnp.dot(inputs_full, in_matrix, preferred_element_type=jnp.float32).astype(
        jnp.bfloat16
    )
    projected = projected.reshape(token_count, 3, channels_dev)
    short_prev = shifted(projected[token_count - STAPS + 1 :], "ctx", 1)
    mixed = tap_sum(jnp.concatenate([short_prev, projected], axis=0), short_taps, token_count, True)
    query, keyed, valued = (mixed[:, 0], mixed[:, 1], mixed[:, 2])
    gated = (keyed * valued).astype(jnp.bfloat16)
    long_prev = shifted(gated[token_count - LTAPS + 1 :], "ctx", 1)
    lower_band, upper_band = make_bands(long_taps)
    gated_tiles = jnp.concatenate(
        [jnp.zeros((1, channels_dev), jnp.bfloat16), long_prev, gated], axis=0
    )
    gated_tiles = gated_tiles.reshape(tile_count + 1, LTAPS, groups_dev, GROUP)
    gated_now = gated_tiles[1:]
    gated_before = gated_tiles[:-1]
    conv_part = jnp.einsum(
        "gab,nbgc->nagc", lower_band, gated_now, preferred_element_type=jnp.float32
    )
    conv_part = conv_part + jnp.einsum(
        "gab,nbgc->nagc", upper_band, gated_before, preferred_element_type=jnp.float32
    )
    wave = conv_part.reshape(token_count, channels_dev) + skip_gain * gated.astype(jnp.float32)
    filtered = (query * wave).astype(jnp.bfloat16)
    out_terms = jnp.dot(filtered, out_proj, preferred_element_type=jnp.float32)
    layer_out = lax.psum_scatter(
        out_terms.astype(jnp.bfloat16), "tp", scatter_dimension=1, tiled=True
    )
    cot_full = lax.all_gather(cotangent, "tp", axis=1, tiled=True)
    grad_filtered = lax.dot_general(
        cot_full, out_proj, (((1,), (1,)), ((), ())), preferred_element_type=jnp.float32
    )
    out_grad_terms = lax.dot_general(
        filtered, cot_full, (((0,), (0,)), ((), ())), preferred_element_type=jnp.float32
    )
    grad_out_proj = lax.psum_scatter(
        out_grad_terms.astype(jnp.bfloat16), "ctx", scatter_dimension=1, tiled=True
    ).astype(jnp.float32)
    grad_wave = (grad_filtered * query).astype(jnp.bfloat16)
    grad_query = grad_filtered * wave
    wave_next = shifted(grad_wave[: LTAPS - 1], "ctx", -1)
    wave_tiles = jnp.concatenate(
        [grad_wave, wave_next, jnp.zeros((1, channels_dev), jnp.bfloat16)], axis=0
    )
    wave_tiles = wave_tiles.reshape(tile_count + 1, LTAPS, groups_dev, GROUP)
    wave_now = wave_tiles[:-1]
    wave_after = wave_tiles[1:]
    back_part = jnp.einsum(
        "gab,nagc->nbgc", lower_band, wave_now, preferred_element_type=jnp.float32
    )
    back_part = back_part + jnp.einsum(
        "gab,nagc->nbgc", upper_band, wave_after, preferred_element_type=jnp.float32
    )
    grad_gated = back_part.reshape(token_count, channels_dev) + skip_gain * grad_wave.astype(
        jnp.float32
    )
    lower_corr = jnp.einsum(
        "nagc,nbgc->gab", wave_now, gated_now, preferred_element_type=jnp.float32
    )
    upper_corr = jnp.einsum(
        "nagc,nbgc->gab", wave_now, gated_before, preferred_element_type=jnp.float32
    )
    lower_sums = lag_totals(lower_corr)
    upper_sums = lag_totals(upper_corr)
    tap_grads = lower_sums[:, LTAPS - 1 :] + jnp.pad(upper_sums[:, : LTAPS - 1], ((0, 0), (1, 0)))
    grad_long_taps = lax.psum(tap_grads.T, "ctx")
    grad_mixed = jnp.stack([grad_query, grad_gated * valued, grad_gated * keyed], axis=1).astype(
        jnp.bfloat16
    )
    mixed_next = shifted(grad_mixed[: STAPS - 1], "ctx", -1)
    grad_projected = tap_sum(
        jnp.concatenate([grad_mixed, mixed_next], axis=0), short_taps, token_count, False
    )
    grad_matrix = grad_projected.astype(jnp.bfloat16).reshape(token_count, 3 * channels_dev)
    input_terms = lax.dot_general(
        grad_matrix, in_matrix, (((1,), (1,)), ((), ())), preferred_element_type=jnp.float32
    )
    grad_inputs = lax.psum_scatter(
        input_terms.astype(jnp.bfloat16), "tp", scatter_dimension=1, tiled=True
    )
    weight_grad = lax.psum_scatter(
        lax.dot_general(
            inputs_full, grad_matrix, (((0,), (0,)), ((), ())), preferred_element_type=jnp.float32
        ).astype(jnp.bfloat16),
        "ctx",
        scatter_dimension=0,
        tiled=True,
    ).astype(jnp.float32)
    grad_in_proj = weight_grad.reshape(weight_grad.shape[0], 3, channels_dev)
    return (layer_out, grad_inputs, grad_in_proj, grad_out_proj, grad_long_taps)


def solution(mesh):
    placed = (
        P("ctx", "tp"),
        P(None, None, "tp"),
        P("tp", None),
        P(None, None, "tp"),
        P("tp"),
        P(None, "tp"),
        P("ctx", "tp"),
    )
    return jax.shard_map(
        local,
        mesh=mesh,
        in_specs=placed,
        out_specs=(
            P("ctx", "tp"),
            P("ctx", "tp"),
            P("ctx", None, "tp"),
            P("tp", "ctx"),
            P(None, "tp"),
        ),
        check_vma=False,
    )
```

profile of v0, /device:TPU:0, one launch (start us, length us, event | category | flops | bytes accessed | tf_op | source)
XLA Modules:
  0.0 505.0 jit_solution(2170695225887025520)
XLA Ops:
  8.7 8.7 %copy.27 = bf16[4096,3,256]{0,2,1:T(8,128)(2,1)} copy(bf16[4096,3,256]{2,0,1:T(8,128)(2,1)} %param.8) | data formatting | bytes 12582912 | tf_op args[1]
  19.7 60.1 %all-gather.3.cloned.1.call-done = bf16[768,4096]{1,0:T(8,128)(2,1)} async-done(((bf16[768,256]{1,0:T(8,128)(2,1)}), bf16[768,4096]{1,0:T(8,128)(2,1)}) %all-gather.3.cloned.1.call-update) | async-done | bytes 6291472 | tf_op jit(solution)/shard_map/all_gather | solution.py:63
  79.8 9.0 %convolution_convert_fusion.3 = bf16[768,768]{1,0:T(8,128)(2,1)S(1)} fusion(bf16[768,4096]{1,0:T(8,128)(2,1)} %all-gather.3.cloned.1.call-done, bf16[4096,768]{0,1:T(8,128)(2,1)} %bitcast.122), kind=kOutput, calls=%fused_computation.18 | convolution fusion | flops 4832428032 | bytes 13762560 | tf_op jit(solution)/shard_map/dot_general | solution.py:64
  88.8 3.4 collective-permute-start
  92.2 2.5 fusion.8
  102.2 44.4 %all-gather.5.cloned.1.call-done = bf16[768,4096]{1,0:T(8,128)(2,1)} async-done(((bf16[768,256]{1,0:T(8,128)(2,1)}), bf16[768,4096]{1,0:T(8,128)(2,1)}) %all-gather.5.cloned.1.call-update) | async-done | bytes 6291472 | tf_op jit(solution)/shard_map/all_gather | solution.py:92
  146.6 6.2 %multiply_convert_fusion = (bf16[768,256]{1,0:T(8,128)(2,1)S(1)}, bf16[768,256]{1,0:T(8,128)(2,1)S(1)}, f32[768,256]{1,0:T(8,128)}) fusion(f32[768,3,256]{2,0,1:T(8,128)} %copy-done.1, bf16[768,4096]{1,0:T(8,128)(2,1)} %all-gather.5.cloned.1.call-done, bf16[256,4096]{1,0:T(8,128)(2,1)S(1)} %copy-done), kind=kOutput, calls=%fused_computation.50 | convolution fusion | flops 1611399168 | bytes 12320768 | tf_op jit(solution)/shard_map/dot_general | solution.py:93
  160.4 4.7 collective-permute-start.1
  185.6 3.0 fusion.26
  189.3 5.9 %convolution_convert_fusion.2 = bf16[256,4096]{1,0:T(8,128)(2,1)} fusion(bf16[768,256]{1,0:T(8,128)(2,1)S(1)} %get-tuple-element.17, bf16[768,4096]{1,0:T(8,128)(2,1)} %all-gather.5.cloned.1.call-done), kind=kOutput, calls=%fused_computation.9 | convolution fusion | flops 1611661312 | bytes 8781824 | tf_op jit(solution)/shard_map/dot_general | solution.py:96
  196.8 4.3 collective-permute-done.3
  201.2 3.0 add_convert_fusion
  205.7 9.7 %fusion.2 = bf16[4096,768]{0,1:T(8,128)(2,1)} fusion(bf16[768,768]{0,1:T(8,128)(2,1)S(1)} %bitcast.128, bf16[768,4096]{1,0:T(8,128)(2,1)} %all-gather.3.cloned.1.call-done), kind=kOutput, calls=%fused_computation.8 | convolution fusion | flops 4834983936 | bytes 13762560 | tf_op jit(solution)/shard_map/dot_general | solution.py:145
  216.5 4.4 convolution_convert_fusion
  222.2 9.7 %bitcast_convert_fusion = bf16[768,4096]{1,0:T(8,128)(2,1)} fusion(bf16[768,3,256]{2,0,1:T(8,128)(2,1)S(1)} %copy-done.4, bf16[4096,3,256]{2,0,1:T(8,128)(2,1)} %param.8), kind=kOutput, calls=%fused_computation | convolution fusion | flops 4834983936 | bytes 13762560 | tf_op jit(solution)/shard_map/dot_general | solution.py:138
  234.4 7.5 %rev.6 = f32[16,128,128]{2,1,0:T(8,128)S(1)} reverse(f32[16,128,128]{2,1,0:T(8,128)} %convolution_bitcast_fusion.1), dimensions={2} | reverse | bytes 2097152 | tf_op jit(solution)/shard_map/rev | solution.py:48
  244.9 6.4 %reshape.63 = f32[16,128,255]{2,1,0:T(8,128)} reshape(f32[16,32640]{1,0:T(8,128)} %slice.177) | data formatting | bytes 4177920 | tf_op jit(solution)/shard_map/reshape | solution.py:53
  254.4 7.5 %rev.7 = f32[16,128,128]{2,1,0:T(8,128)S(1)} reverse(f32[16,128,128]{2,1,0:T(8,128)} %convolution_bitcast_fusion), dimensions={2} | reverse | bytes 2097152 | tf_op jit(solution)/shard_map/rev | solution.py:48
  264.9 6.2 %reshape.65 = f32[16,128,255]{2,1,0:T(8,128)} reshape(f32[16,32640]{1,0:T(8,128)} %slice.179) | data formatting | bytes 4177920 | tf_op jit(solution)/shard_map/reshape | solution.py:53
  272.9 22.4 %psum.7 = f32[128,16]{0,1:T(8,128)} all-reduce(f32[128,16]{0,1:T(8,128)S(1)} %fusion.35), channel_id=1, replica_groups=mesh['ctx'=8,'tp'=16] {'ctx'}, use_global_device_ids=true, to_apply=%region_6.7 | all-reduce | flops 2048 | bytes 16384 | tf_op jit(solution)/shard_map/psum | solution.py:129
  297.1 14.2 %reduce-scatter.9.cloned.1.call-done = bf16[512,768]{0,1:T(8,128)(2,1)} async-done(((bf16[4096,768]{0,1:T(8,128)(2,1)}), bf16[512,768]{0,1:T(8,128)(2,1)}) %reduce-scatter.9.cloned.1.call-update) | async-done | bytes 786448 | tf_op jit(solution)/shard_map/reduce_scatter | solution.py:144
  311.3 2.5 copy.53
  313.9 90.6 %reduce-scatter.5.cloned.1.call-done = bf16[768,256]{1,0:T(8,128)(2,1)} async-done(((bf16[768,4096]{1,0:T(8,128)(2,1)}), bf16[768,256]{1,0:T(8,128)(2,1)}) %reduce-scatter.5.cloned.1.call-update) | async-done | bytes 393232 | tf_op jit(solution)/shard_map/reduce_scatter | solution.py:89
  404.5 93.7 %reduce-scatter.7.cloned.1.call-done = bf16[768,256]{1,0:T(8,128)(2,1)} async-done(((bf16[768,4096]{1,0:T(8,128)(2,1)}), bf16[768,256]{1,0:T(8,128)(2,1)}) %reduce-scatter.7.cloned.1.call-update) | async-done | bytes 393232 | tf_op jit(solution)/shard_map/reduce_scatter | solution.py:141
  (114 shorter events, 60.4 us)
Async XLA Ops:
  7.2 139.4 %copy-start = (bf16[256,4096]{1,0:T(8,128)(2,1)S(1)}, bf16[256,4096]{1,0:T(8,128)(2,1)}, u32[]{:S(2)}) copy-start(bf16[256,4096]{1,0:T(8,128)(2,1)} %param.9) | copy-start | bytes 6291460
  7.2 72.6 %all-gather.3.cloned.1.call-start = ((), (), s32[]{:S(2)}) async-start(), calls=%async_computation.4 | async-start | bytes 6684672 | tf_op jit(solution)/shard_map/all_gather | solution.py:63
  7.9 138.7 %all-gather.5.cloned.1.call-start = ((), (), s32[]{:S(2)}) async-start(), calls=%async_computation.6 | async-start | bytes 6684672 | tf_op jit(solution)/shard_map/all_gather | solution.py:92
  8.7 8.8 %copy-start.20 = (f32[7,3,256]{2,0,1:T(8,128)S(1)}, f32[7,3,256]{2,0,1:T(8,128)}, u32[]{:S(2)}) copy-start(f32[7,3,256]{2,0,1:T(8,128)} %param.10) | copy-start | bytes 64516
  8.7 8.8 %copy-start.22 = (bf16[128,16]{0,1:T(8,128)(2,1)S(1)}, bf16[128,16]{0,1:T(8,128)(2,1)}, u32[]{:S(2)}) copy-start(bf16[128,16]{0,1:T(8,128)(2,1)} %param.12) | copy-start | bytes 12292
  8.7 286.6 %reduce-scatter.11.cloned.1.call-start = ((), (), s32[]{:S(2)}) async-start(), calls=%async_computation.9 | async-start | bytes 2359296 | tf_op jit(solution)/shard_map/reduce_scatter | solution.py:99
  17.5 80.3 %copy-start.14 = (f32[3,256]{1,0:T(4,128)}, f32[3,256]{1,0:T(4,128)S(1)}, u32[]{:S(2)}) copy-start(f32[3,256]{1,0:T(4,128)S(1)} %get-tuple-element.31) | copy-start | bytes 9220
  17.5 80.3 %copy-start.16 = (f32[3,256]{1,0:T(4,128)}, f32[3,256]{1,0:T(4,128)S(1)}, u32[]{:S(2)}) copy-start(f32[3,256]{1,0:T(4,128)S(1)} %get-tuple-element.32) | copy-start | bytes 9220
  88.8 8.9 %collective-permute-start = (bf16[6,3,256]{2,0,1:T(8,128)(2,1)S(1)}, bf16[6,3,256]{2,0,1:T(8,128)(2,1)S(1)}, u32[]{:S(2)}, u32[]{:S(2)}) collective-permute-start(bf16[6,3,256]{2,0,1:T(8,128)(2,1)S(1)} %bitcast.132), channel_id=1, source_target_pairs={{0,16},{16,32},{32,48},{48,64},{64,80},{80,96},{96,112},{1,17},{17... | collective-permute-start | bytes 27656 | tf_op jit(solution)/shard_map/ppermute | solution.py:14
  152.8 14.6 %copy-start.8 = (bf16[768,256]{1,0:T(8,128)(2,1)}, bf16[768,256]{1,0:T(8,128)(2,1)S(1)}, u32[]{:S(2)}) copy-start(bf16[768,256]{1,0:T(8,128)(2,1)S(1)} %get-tuple-element.19) | copy-start | bytes 1179652
  152.8 18.6 %copy-start.5 = (bf16[768,256]{1,0:T(8,128)(2,1)}, bf16[768,256]{1,0:T(8,128)(2,1)S(1)}, u32[]{:S(2)}) copy-start(bf16[768,256]{1,0:T(8,128)(2,1)S(1)} %get-tuple-element.18) | copy-start | bytes 1179652
  152.8 14.6 %copy-start.7 = (bf16[16,128,128,1]{2,0,1,3:T(8,128)(2,1)S(1)}, bf16[16,128,128,1]{2,0,1,3:T(8,128)(2,1)}, u32[]{:S(2)}) copy-start(bf16[16,128,128,1]{2,0,1,3:T(8,128)(2,1)} %fusion.8) | copy-start | bytes 1572868
  159.1 12.2 %collective-permute-start.2 = (bf16[127,256]{1,0:T(8,128)(2,1)}, bf16[127,256]{1,0:T(8,128)(2,1)S(1)}, u32[]{:S(2)}, u32[]{:S(2)}) collective-permute-start(bf16[127,256]{1,0:T(8,128)(2,1)} %slice.169), channel_id=1, source_target_pairs={{16,0},{32,16},{48,32},{64,48},{80,64},{96,80},{112,96},{17,1},{33... | collective-permute-start | bytes 195080 | tf_op jit(solution)/shard_map/ppermute | solution.py:14
  160.4 10.9 %collective-permute-start.1 = (bf16[127,256]{1,0:T(8,128)(2,1)}, bf16[127,256]{1,0:T(8,128)(2,1)S(1)}, u32[]{:S(2)}, u32[]{:S(2)}) collective-permute-start(bf16[127,256]{1,0:T(8,128)(2,1)} %slice.168), channel_id=1, source_target_pairs={{0,16},{16,32},{32,48},{48,64},{64,80},{80,96},{96,112},{1,17},{17... | collective-permute-start | bytes 195080 | tf_op jit(solution)/shard_map/ppermute | solution.py:14
  177.4 4.7 copy-start.6
  195.2 116.1 %reduce-scatter.9.cloned.1.call-start = ((), (), s32[]{:S(2)}) async-start(), calls=%async_computation.8 | async-start | bytes 7077888 | tf_op jit(solution)/shard_map/reduce_scatter | solution.py:144
  195.3 5.9 %copy-start.15 = (f32[3,256]{1,0:T(4,128)S(1)}, f32[3,256]{1,0:T(4,128)}, u32[]{:S(2)}) copy-start(f32[3,256]{1,0:T(4,128)} %copy-done.14) | copy-start | bytes 9220
  195.3 5.9 %copy-start.17 = (f32[3,256]{1,0:T(4,128)S(1)}, f32[3,256]{1,0:T(4,128)}, u32[]{:S(2)}) copy-start(f32[3,256]{1,0:T(4,128)} %copy-done.16) | copy-start | bytes 9220
  195.3 5.9 %copy-start.19 = (f32[1,3,256]{2,1,0:T(4,128)S(1)}, f32[1,3,256]{2,1,0:T(4,128)}, u32[]{:S(2)}) copy-start(f32[1,3,256]{2,1,0:T(4,128)} %copy-done.18) | copy-start | bytes 9220
  195.5 5.6 %collective-permute-start.3 = (bf16[6,3,256]{2,0,1:T(8,128)(2,1)S(1)}, bf16[6,3,256]{2,0,1:T(8,128)(2,1)S(1)}, u32[]{:S(2)}, u32[]{:S(2)}) collective-permute-start(bf16[6,3,256]{2,0,1:T(8,128)(2,1)S(1)} %slice.170), channel_id=1, source_target_pairs={{16,0},{32,16},{48,32},{64,48},{80,64},{96,80},{112,96},{17,1},{33... | collective-permute-start | bytes 27656 | tf_op jit(solution)/shard_map/ppermute | solution.py:14
  215.5 189.0 %reduce-scatter.5.cloned.1.call-start = ((), (), s32[]{:S(2)}) async-start(), calls=%async_computation.5 | async-start | bytes 6684672 | tf_op jit(solution)/shard_map/reduce_scatter | solution.py:89
  220.9 277.3 %reduce-scatter.7.cloned.1.call-start = ((), (), s32[]{:S(2)}) async-start(), calls=%async_computation.7 | async-start | bytes 6684672 | tf_op jit(solution)/shard_map/reduce_scatter | solution.py:141
  244.9 8.1 %copy-start.10 = (bf16[6,128,16,16]{1,0,3,2:T(8,128)(2,1)S(1)}, bf16[6,128,16,16]{1,0,3,2:T(8,128)(2,1)}, u32[]{:S(2)}) copy-start(bf16[6,128,16,16]{1,0,3,2:T(8,128)(2,1)} %copy-done.9) | copy-start | bytes 1179652
  244.9 8.1 %copy-start.12 = (bf16[6,128,16,16]{1,0,3,2:T(8,128)(2,1)S(1)}, bf16[6,128,16,16]{1,0,3,2:T(8,128)(2,1)}, u32[]{:S(2)}) copy-start(bf16[6,128,16,16]{1,0,3,2:T(8,128)(2,1)} %slice.139) | copy-start | bytes 1179652
  (9 other events, 13.4 us)
Sparse Core Ops, SparseCore 0:
  10.4 69.3 all-gather.2
  82.1 64.4 all-gather.4
  195.4 41.2 reduce-scatter.10
  239.0 72.3 reduce-scatter.8
  316.0 88.4 reduce-scatter.4
  409.7 88.4 reduce-scatter.6
where the time goes:
time: 507 us; the launch traced here: 505 us
  waiting for transfers between devices  309 us (61%)
  local copies, waits for them, and re-layouts  72.2 us (14%)
  matrix products  59.6 us (12%)
  blocking collectives  22.4 us (4%)
  other arithmetic  16.4 us (3%)
  between operations  14.6 us (3%)
  starting transfers between devices  11.1 us (2%)
    reduce_scatter x1, waiting for transfers between devices, local(): lax.psum_scatter(input_terms.astype(jnp.bfloat16), 'tp', scatter_dimensio...  93.7 us
    reduce_scatter x1, waiting for transfers between devices, local(): lax.psum_scatter(out_terms.astype(jnp.bfloat16), 'tp', scatter_dimension=...  90.6 us
    all_gather x1, waiting for transfers between devices, local(): inputs_full = lax.all_gather(inputs, 'tp', axis=1, tiled=True)  60.1 us
    all_gather x1, waiting for transfers between devices, local(): cot_full = lax.all_gather(cotangent, 'tp', axis=1, tiled=True)  44.4 us
    psum x1, blocking collectives, local(): grad_long_taps = lax.psum(tap_grads.T, 'ctx')  22.4 us
    unnamed x56, local copies, waits for them, and re-layouts  19.3 us
    rev x2, local copies, waits for them, and re-layouts, lag_totals(): flipped = matrix[:, :, ::-1]  15 us
    reduce_scatter x1, waiting for transfers between devices, local(): lax.psum_scatter(lax.dot_general(inputs_full, grad_matrix, (((0,), (0,)),...  14.2 us
  transfers between devices with their start and end apart: 10, of which 6 were waited for; matrix products, arithmetic and copies ran while one was open for 21% of the time, Pallas kernels for 0%

commit v1 on v0

--- a/solution.py
+++ b/solution.py
@@ -6,6 +6,13 @@
 GROUP = 16
 LTAPS = 128
 STAPS = 7
+
+
+def divide_racks(q_in, which_axis):
+    piece_next = lax.all_to_all(
+        jnp.stack([q_in for _ in range(lax.axis_size(which_axis))]), which_axis, 0, 0
+    )
+    return jnp.concatenate(piece_next, 1)
 
 
 def shifted(shard, axis, by):
@@ -60,7 +67,7 @@
     groups_dev = long_taps.shape[1]
     tile_count = token_count // LTAPS
     in_matrix = in_proj.reshape(model_width, 3 * channels_dev)
-    inputs_full = lax.all_gather(inputs, "tp", axis=1, tiled=True)
+    inputs_full = divide_racks(inputs, "tp")
     projected = jnp.dot(inputs_full, in_matrix, preferred_element_type=jnp.float32).astype(
         jnp.bfloat16
     )

time: 507 us -> 482 us (0.951)
  waiting for transfers between devices: 309 us -> 279 us
  starting transfers between devices: 11.1 us -> 19.3 us
    all_to_all x0 -> x1, waiting for transfers between devices: none -> 67.2 us  [divide_racks(): lax.all_to_all(jnp.stack([q_in for _ in range(lax.axis_size(which_axis))]...]
    all_gather x1 -> x0, waiting for transfers between devices: 60.1 us -> none  [local(): inputs_full = lax.all_gather(inputs, 'tp', axis=1, tiled=True)]
    all_gather x1, waiting for transfers between devices: 44.4 us -> 7.34 us  [local(): cot_full = lax.all_gather(cotangent, 'tp', axis=1, tiled=True)]
    all_to_all x0 -> x1, starting transfers between devices: none -> 8.18 us  [divide_racks(): lax.all_to_all(jnp.stack([q_in for _ in range(lax.axis_size(which_axis))]...]
    unnamed x56 -> x59, local copies, waits for them, and re-layouts: 19.3 us -> 21 us
  transfers between devices with their start and end apart: 10 -> 10, of which waited for: 6 -> 6; matrix products, arithmetic and copies ran while one was open for 21% -> 23% of each run, Pallas kernels for 0% -> 0%
where the time goes in v1:
time: 482 us; the launch traced here: 480 us
  waiting for transfers between devices  279 us (58%)
  local copies, waits for them, and re-layouts  70.5 us (15%)
  matrix products  58.9 us (12%)
  blocking collectives  22.2 us (5%)
  starting transfers between devices  19.3 us (4%)
  other arithmetic  15.7 us (3%)
  between operations  14.3 us (3%)
    reduce_scatter x1, waiting for transfers between devices, local(): lax.psum_scatter(input_terms.astype(jnp.bfloat16), 'tp', scatter_dimensio...  93.8 us
    reduce_scatter x1, waiting for transfers between devices, local(): lax.psum_scatter(out_terms.astype(jnp.bfloat16), 'tp', scatter_dimension=...  90.6 us
    all_to_all x1, waiting for transfers between devices, divide_racks(): lax.all_to_all(jnp.stack([q_in for _ in range(lax.axis_size(which_axis))]...  67.2 us
    psum x1, blocking collectives, local(): grad_long_taps = lax.psum(tap_grads.T, 'ctx')  22.2 us
    unnamed x59, local copies, waits for them, and re-layouts  21 us
    rev x2, local copies, waits for them, and re-layouts, lag_totals(): flipped = matrix[:, :, ::-1]  15 us
    reduce_scatter x1, waiting for transfers between devices, local(): lax.psum_scatter(lax.dot_general(inputs_full, grad_matrix, (((0,), (0,)),...  14.9 us
    reshape x2, local copies, waits for them, and re-layouts, lag_totals(): flat_rows.reshape(group_count, tap_count, 2 * tap_count - 1).sum(axis=1)  12.5 us
  transfers between devices with their start and end apart: 10, of which 6 were waited for; matrix products, arithmetic and copies ran while one was open for 23% of the time, Pallas kernels for 0%

profile of v1, /device:TPU:0, one launch (start us, length us, event | category | flops | bytes accessed | tf_op | source)
XLA Modules:
  0.0 479.9 jit_solution(611897426589506231)
XLA Ops:
  9.1 3.2 stack.14
  12.3 8.2 %all-to-all-start = ((bf16[16,768,256]{1,2,0:T(8,128)(2,1)}), bf16[16,768,256]{1,2,0:T(8,128)(2,1)}, u32[]{:S(2)}, u32[]{:S(2)}) async-start(bf16[16,768,256]{1,2,0:T(8,128)(2,1)} %stack.14), calls=%async_computation | async-start | bytes 12582912 | tf_op jit(solution)/shard_map/all_to_all | solution.py:12
  20.6 8.9 %copy.28 = bf16[4096,3,256]{0,2,1:T(8,128)(2,1)} copy(bf16[4096,3,256]{2,0,1:T(8,128)(2,1)} %param.8) | data formatting | bytes 12582912 | tf_op args[1]
  31.8 67.2 %all-to-all-done = bf16[16,768,256]{1,2,0:T(8,128)(2,1)} async-done(((bf16[16,768,256]{1,2,0:T(8,128)(2,1)}), bf16[16,768,256]{1,2,0:T(8,128)(2,1)}, u32[]{:S(2)}, u32[]{:S(2)}) %all-to-all-start) | async-done | bytes 6291488 | tf_op jit(solution)/shard_map/all_to_all | solution.py:12
  99.0 9.3 %convolution_convert_fusion.3 = bf16[768,768]{1,0:T(8,128)(2,1)S(1)} fusion(bf16[768,4096]{0,1:T(8,128)(2,1)} %bitcast.1, bf16[4096,768]{0,1:T(8,128)(2,1)} %bitcast.125), kind=kOutput, calls=%fused_computation.18 | convolution fusion | flops 4832428032 | bytes 13762560 | tf_op jit(solution)/shard_map/dot_general | solution.py:71
  108.3 3.4 collective-permute-start
  123.3 7.3 %all-gather.2.cloned.1.call-done = bf16[768,4096]{1,0:T(8,128)(2,1)} async-done(((bf16[768,256]{1,0:T(8,128)(2,1)}), bf16[768,4096]{1,0:T(8,128)(2,1)}) %all-gather.2.cloned.1.call-update) | async-done | bytes 6291472 | tf_op jit(solution)/shard_map/all_gather | solution.py:99
  130.7 6.2 %multiply_convert_fusion = (bf16[768,256]{1,0:T(8,128)(2,1)S(1)}, bf16[768,256]{1,0:T(8,128)(2,1)S(1)}, f32[768,256]{1,0:T(8,128)}) fusion(f32[768,3,256]{2,0,1:T(8,128)} %copy-done.1, bf16[768,4096]{1,0:T(8,128)(2,1)} %all-gather.2.cloned.1.call-done, bf16[256,4096]{1,0:T(8,128)(2,1)S(1)} %copy-done), kind=kOutput, calls=%fused_computation.50 | convolution fusion | flops 1611399168 | bytes 12320768 | tf_op jit(solution)/shard_map/dot_general | solution.py:100
  138.3 4.7 collective-permute-start.1
  160.1 3.0 fusion.26
  163.8 5.9 %convolution_convert_fusion.2 = bf16[256,4096]{1,0:T(8,128)(2,1)} fusion(bf16[768,256]{1,0:T(8,128)(2,1)S(1)} %get-tuple-element.17, bf16[768,4096]{1,0:T(8,128)(2,1)} %all-gather.2.cloned.1.call-done), kind=kOutput, calls=%fused_computation.9 | convolution fusion | flops 1611661312 | bytes 8781824 | tf_op jit(solution)/shard_map/dot_general | solution.py:103
  171.3 4.3 collective-permute-done.3
  175.7 3.0 add_convert_fusion
  180.3 9.8 %fusion.2 = bf16[4096,768]{0,1:T(8,128)(2,1)} fusion(bf16[768,768]{0,1:T(8,128)(2,1)S(1)} %bitcast.131, bf16[768,4096]{0,1:T(8,128)(2,1)} %bitcast.1), kind=kOutput, calls=%fused_computation.8 | convolution fusion | flops 4834983936 | bytes 13762560 | tf_op jit(solution)/shard_map/dot_general | solution.py:152
  191.0 4.4 convolution_convert_fusion
  196.7 9.7 %bitcast_convert_fusion = bf16[768,4096]{1,0:T(8,128)(2,1)} fusion(bf16[768,3,256]{2,0,1:T(8,128)(2,1)S(1)} %copy-done.4, bf16[4096,3,256]{2,0,1:T(8,128)(2,1)} %param.8), kind=kOutput, calls=%fused_computation | convolution fusion | flops 4834983936 | bytes 13762560 | tf_op jit(solution)/shard_map/dot_general | solution.py:145
  209.0 7.5 %rev.6 = f32[16,128,128]{2,1,0:T(8,128)S(1)} reverse(f32[16,128,128]{2,1,0:T(8,128)} %convolution_bitcast_fusion.1), dimensions={2} | reverse | bytes 2097152 | tf_op jit(solution)/shard_map/rev | solution.py:55
  219.5 6.3 %reshape.73 = f32[16,128,255]{2,1,0:T(8,128)} reshape(f32[16,32640]{1,0:T(8,128)} %slice.177) | data formatting | bytes 4177920 | tf_op jit(solution)/shard_map/reshape | solution.py:60
  228.9 7.5 %rev.7 = f32[16,128,128]{2,1,0:T(8,128)S(1)} reverse(f32[16,128,128]{2,1,0:T(8,128)} %convolution_bitcast_fusion), dimensions={2} | reverse | bytes 2097152 | tf_op jit(solution)/shard_map/rev | solution.py:55
  239.4 6.2 %reshape.75 = f32[16,128,255]{2,1,0:T(8,128)} reshape(f32[16,32640]{1,0:T(8,128)} %slice.179) | data formatting | bytes 4177920 | tf_op jit(solution)/shard_map/reshape | solution.py:60
  247.5 22.2 %psum.7 = f32[128,16]{0,1:T(8,128)} all-reduce(f32[128,16]{0,1:T(8,128)S(1)} %fusion.35), channel_id=1, replica_groups=mesh['ctx'=8,'tp'=16] {'ctx'}, use_global_device_ids=true, to_apply=%region_6.7 | all-reduce | flops 2048 | bytes 16384 | tf_op jit(solution)/shard_map/psum | solution.py:136
  271.5 14.9 %reduce-scatter.9.cloned.1.call-done = bf16[512,768]{0,1:T(8,128)(2,1)} async-done(((bf16[4096,768]{0,1:T(8,128)(2,1)}), bf16[512,768]{0,1:T(8,128)(2,1)}) %reduce-scatter.9.cloned.1.call-update) | async-done | bytes 786448 | tf_op jit(solution)/shard_map/reduce_scatter | solution.py:151
  289.0 90.6 %reduce-scatter.5.cloned.1.call-done = bf16[768,256]{1,0:T(8,128)(2,1)} async-done(((bf16[768,4096]{1,0:T(8,128)(2,1)}), bf16[768,256]{1,0:T(8,128)(2,1)}) %reduce-scatter.5.cloned.1.call-update) | async-done | bytes 393232 | tf_op jit(solution)/shard_map/reduce_scatter | solution.py:96
  379.6 93.8 %reduce-scatter.7.cloned.1.call-done = bf16[768,256]{1,0:T(8,128)(2,1)} async-done(((bf16[768,4096]{1,0:T(8,128)(2,1)}), bf16[768,256]{1,0:T(8,128)(2,1)}) %reduce-scatter.7.cloned.1.call-update) | async-done | bytes 393232 | tf_op jit(solution)/shard_map/reduce_scatter | solution.py:148
  (117 shorter events, 58.0 us)
Async XLA Ops:
  7.2 123.5 %copy-start = (bf16[256,4096]{1,0:T(8,128)(2,1)S(1)}, bf16[256,4096]{1,0:T(8,128)(2,1)}, u32[]{:S(2)}) copy-start(bf16[256,4096]{1,0:T(8,128)(2,1)} %param.9) | copy-start | bytes 6291460
  7.2 123.5 %all-gather.2.cloned.1.call-start = ((), (), s32[]{:S(2)}) async-start(), calls=%async_computation.6 | async-start | bytes 6684672 | tf_op jit(solution)/shard_map/all_gather | solution.py:99
  12.3 86.7 %all-to-all-start = ((bf16[16,768,256]{1,2,0:T(8,128)(2,1)}), bf16[16,768,256]{1,2,0:T(8,128)(2,1)}, u32[]{:S(2)}, u32[]{:S(2)}) async-start(bf16[16,768,256]{1,2,0:T(8,128)(2,1)} %stack.14), calls=%async_computation | async-start | bytes 12582912 | tf_op jit(solution)/shard_map/all_to_all | solution.py:12
  20.5 9.0 %copy-start.21 = (f32[7,3,256]{2,0,1:T(8,128)S(1)}, f32[7,3,256]{2,0,1:T(8,128)}, u32[]{:S(2)}) copy-start(f32[7,3,256]{2,0,1:T(8,128)} %param.10) | copy-start | bytes 64516
  20.5 9.0 %copy-start.23 = (bf16[128,16]{0,1:T(8,128)(2,1)S(1)}, bf16[128,16]{0,1:T(8,128)(2,1)}, u32[]{:S(2)}) copy-start(bf16[128,16]{0,1:T(8,128)(2,1)} %param.12) | copy-start | bytes 12292
  20.5 249.2 %reduce-scatter.11.cloned.1.call-start = ((), (), s32[]{:S(2)}) async-start(), calls=%async_computation.9 | async-start | bytes 2359296 | tf_op jit(solution)/shard_map/reduce_scatter | solution.py:106
  29.5 87.8 %copy-start.15 = (f32[3,256]{1,0:T(4,128)}, f32[3,256]{1,0:T(4,128)S(1)}, u32[]{:S(2)}) copy-start(f32[3,256]{1,0:T(4,128)S(1)} %get-tuple-element.31) | copy-start | bytes 9220
  29.5 87.8 %copy-start.17 = (f32[3,256]{1,0:T(4,128)}, f32[3,256]{1,0:T(4,128)S(1)}, u32[]{:S(2)}) copy-start(f32[3,256]{1,0:T(4,128)S(1)} %get-tuple-element.32) | copy-start | bytes 9220
  108.3 9.0 %collective-permute-start = (bf16[6,3,256]{2,0,1:T(8,128)(2,1)S(1)}, bf16[6,3,256]{2,0,1:T(8,128)(2,1)S(1)}, u32[]{:S(2)}, u32[]{:S(2)}) collective-permute-start(bf16[6,3,256]{2,0,1:T(8,128)(2,1)S(1)} %bitcast.135), channel_id=1, source_target_pairs={{0,16},{16,32},{32,48},{48,64},{64,80},{80,96},{96,112},{1,17},{17... | collective-permute-start | bytes 27656 | tf_op jit(solution)/shard_map/ppermute | solution.py:21
  114.3 3.0 copy-start.19
  136.8 6.3 %copy-start.8 = (bf16[768,256]{1,0:T(8,128)(2,1)}, bf16[768,256]{1,0:T(8,128)(2,1)S(1)}, u32[]{:S(2)}) copy-start(bf16[768,256]{1,0:T(8,128)(2,1)S(1)} %get-tuple-element.19) | copy-start | bytes 1179652
  136.8 10.9 %copy-start.5 = (bf16[768,256]{1,0:T(8,128)(2,1)}, bf16[768,256]{1,0:T(8,128)(2,1)S(1)}, u32[]{:S(2)}) copy-start(bf16[768,256]{1,0:T(8,128)(2,1)S(1)} %get-tuple-element.18) | copy-start | bytes 1179652
  137.0 8.8 %collective-permute-start.2 = (bf16[127,256]{1,0:T(8,128)(2,1)S(1)}, bf16[127,256]{1,0:T(8,128)(2,1)S(1)}, u32[]{:S(2)}, u32[]{:S(2)}) collective-permute-start(bf16[127,256]{1,0:T(8,128)(2,1)S(1)} %slice.169), channel_id=1, source_target_pairs={{16,0},{32,16},{48,32},{64,48},{80,64},{96,80},{112,96},{17,1},{33... | collective-permute-start | bytes 195080 | tf_op jit(solution)/shard_map/ppermute | solution.py:21
  138.3 7.5 %collective-permute-start.1 = (bf16[127,256]{1,0:T(8,128)(2,1)S(1)}, bf16[127,256]{1,0:T(8,128)(2,1)S(1)}, u32[]{:S(2)}, u32[]{:S(2)}) collective-permute-start(bf16[127,256]{1,0:T(8,128)(2,1)S(1)} %slice.168), channel_id=1, source_target_pairs={{0,16},{16,32},{32,48},{48,64},{64,80},{80,96},{96,112},{1,17},{17... | collective-permute-start | bytes 195080 | tf_op jit(solution)/shard_map/ppermute | solution.py:21
  151.9 4.7 copy-start.6
  169.8 116.7 %reduce-scatter.9.cloned.1.call-start = ((), (), s32[]{:S(2)}) async-start(), calls=%async_computation.8 | async-start | bytes 7077888 | tf_op jit(solution)/shard_map/reduce_scatter | solution.py:151
  169.8 5.9 %copy-start.16 = (f32[3,256]{1,0:T(4,128)S(1)}, f32[3,256]{1,0:T(4,128)}, u32[]{:S(2)}) copy-start(f32[3,256]{1,0:T(4,128)} %copy-done.15) | copy-start | bytes 9220
  169.8 5.9 %copy-start.18 = (f32[3,256]{1,0:T(4,128)S(1)}, f32[3,256]{1,0:T(4,128)}, u32[]{:S(2)}) copy-start(f32[3,256]{1,0:T(4,128)} %copy-done.17) | copy-start | bytes 9220
  169.8 5.9 %copy-start.20 = (f32[1,3,256]{2,1,0:T(4,128)S(1)}, f32[1,3,256]{2,1,0:T(4,128)}, u32[]{:S(2)}) copy-start(f32[1,3,256]{2,1,0:T(4,128)} %copy-done.19) | copy-start | bytes 9220
  170.0 5.6 %collective-permute-start.3 = (bf16[6,3,256]{2,0,1:T(8,128)(2,1)S(1)}, bf16[6,3,256]{2,0,1:T(8,128)(2,1)S(1)}, u32[]{:S(2)}, u32[]{:S(2)}) collective-permute-start(bf16[6,3,256]{2,0,1:T(8,128)(2,1)S(1)} %slice.170), channel_id=1, source_target_pairs={{16,0},{32,16},{48,32},{64,48},{80,64},{96,80},{112,96},{17,1},{33... | collective-permute-start | bytes 27656 | tf_op jit(solution)/shard_map/ppermute | solution.py:21
  190.0 189.6 %reduce-scatter.5.cloned.1.call-start = ((), (), s32[]{:S(2)}) async-start(), calls=%async_computation.5 | async-start | bytes 6684672 | tf_op jit(solution)/shard_map/reduce_scatter | solution.py:96
  195.5 277.9 %reduce-scatter.7.cloned.1.call-start = ((), (), s32[]{:S(2)}) async-start(), calls=%async_computation.7 | async-start | bytes 6684672 | tf_op jit(solution)/shard_map/reduce_scatter | solution.py:148
  219.5 8.1 %copy-start.10 = (bf16[6,128,16,16]{1,0,3,2:T(8,128)(2,1)S(1)}, bf16[6,128,16,16]{1,0,3,2:T(8,128)(2,1)}, u32[]{:S(2)}) copy-start(bf16[6,128,16,16]{1,0,3,2:T(8,128)(2,1)} %copy-done.9) | copy-start | bytes 1179652
  219.5 8.1 %copy-start.14 = (bf16[6,128,16,16]{1,0,3,2:T(8,128)(2,1)S(1)}, bf16[6,128,16,16]{1,0,3,2:T(8,128)(2,1)}, u32[]{:S(2)}) copy-start(bf16[6,128,16,16]{1,0,3,2:T(8,128)(2,1)} %slice.139) | copy-start | bytes 1179652
  (10 other events, 12.8 us)
Sparse Core Ops, SparseCore 0:
  10.4 120.2 all-gather.1
  169.9 41.7 reduce-scatter.10
  214.1 72.3 reduce-scatter.8
  291.0 88.5 reduce-scatter.4
  384.8 88.5 reduce-scatter.6
